TPU v7x, 32 devices: a whole 2x2x4 slice. The times are simulated.
32 devices in a mesh: dp: 8 (over z, x), rows: 4 (over y, core).
Axes of the slice: x: 2, y: 2, z: 4, core: 2. Of those that a mesh axis runs over, the one named last changes fastest.
Arguments:
- token_ids: int32 [32, 128], P(('dp', 'rows')), may hold values from 0 to 4095, as said below
- upstream: bfloat16 [32, 128, 5376], P(('dp', 'rows')), may hold values from -6 to 6
- saved_rows: bfloat16 [32, 128, 5376], P(('dp', 'rows')), may hold values from -4 to 4
- norm_gain: float32 [5376], replicated, may hold values from 0.5 to 1.5
- master: float32 [4096, 5376], P('rows', 'dp'), may hold values from -6 to 6
- moment_one: float32 [4096, 5376], P('rows', 'dp'), may hold values from -4 to 4
- moment_two: float32 [4096, 5376], P('rows', 'dp'), may hold values from 0.1 to 4
Outputs:
- master_new: float32 [4096, 5376], P('rows', 'dp')
- moment_one_new: float32 [4096, 5376], P('rows', 'dp')
- moment_two_new: float32 [4096, 5376], P('rows', 'dp')
- new_rows: bfloat16 [32, 128, 5376], P(('dp', 'rows'))
Inputs may be any that keep to these rules, and one draw needn't show every extreme that they name: `token_ids`: rows v with v // 1024 = k belong to owner k. In each sequence, one owner receives exactly 32 of its tokens and every other owner at most 32.
All inputs are finite; a program needn't handle non-finite values.
Results may differ from a plain program's by a relative error of at most 0.007.
Values may be sent and summed in bfloat16 or wider, within the bound.
No kernel may reach another device: no remote copies, remote signals or barrier semaphores. Data moves between devices by JAX's collectives and lax.ppermute only.
A program may use at most 64 MiB of HBM per device.

v0:
```python
import math

import jax
import jax.numpy as jnp
from jax import lax
from jax.sharding import PartitionSpec as P


def norm_back(upstream_rows, saved, gain):
    values = saved.astype(jnp.float32)
    row_mean = jnp.mean(values, axis=-1, keepdims=True)
    centered = values - row_mean
    variance = jnp.mean(centered * centered, axis=-1, keepdims=True)
    inv_std = lax.rsqrt(variance + 1e-05)
    normed = centered * inv_std
    scaled = upstream_rows.astype(jnp.float32) * gain
    mean_scaled = jnp.mean(scaled, axis=-1, keepdims=True)
    mean_cross = jnp.mean(scaled * normed, axis=-1, keepdims=True)
    return (inv_std * (scaled - mean_scaled - normed * mean_cross)).astype(jnp.bfloat16)


def per_device(token_ids, upstream, saved_rows, norm_gain, master, moment_one, moment_two):
    owned_rows = master.shape[0]
    slice_width = master.shape[1]
    seq_tokens = token_ids.shape[1]
    group_ids = lax.all_gather(token_ids, "dp", axis=0, tiled=True)
    row_input = norm_back(upstream[0], saved_rows[0], norm_gain)[None]
    slices = lax.all_to_all(row_input, "dp", split_axis=2, concat_axis=0, tiled=True)
    row_iota = lax.iota(jnp.int32, owned_rows)
    owners = lax.axis_size("rows")
    seq_count = slices.shape[0]
    capacity = seq_tokens // 4
    owner = group_ids // owned_rows
    local = group_ids - owner * owned_rows
    owner_hot = (owner[:, :, None] == lax.iota(jnp.int32, owners)[None, None, :]).astype(jnp.int32)
    before = jnp.cumsum(owner_hot, axis=1) - owner_hot
    slot_rank = jnp.sum(before * owner_hot, axis=2)
    target = owner * capacity + slot_rank
    placed = target[:, None, :] == lax.iota(jnp.int32, owners * capacity)[None, :, None]
    buckets = jnp.einsum(
        "sct,std->scd", placed.astype(jnp.bfloat16), slices, preferred_element_type=jnp.float32
    ).astype(jnp.bfloat16)
    bucket_ids = jnp.sum(jnp.where(placed, local[:, None, :] + 1, 0), axis=2) - 1
    buckets = buckets.reshape(seq_count, owners, capacity, slice_width)
    bucket_ids = bucket_ids.reshape(seq_count, owners, capacity)
    arrived, arrived_ids = (
        lax.all_to_all(buckets, "rows", split_axis=1, concat_axis=1, tiled=True),
        lax.all_to_all(bucket_ids, "rows", split_axis=1, concat_axis=1, tiled=True),
    )
    group_size = math.gcd(seq_count, 8)
    grouped_grad = arrived.reshape(
        seq_count // group_size, group_size * owners * capacity, slice_width
    )
    grouped_ids = arrived_ids.reshape(seq_count // group_size, group_size * owners * capacity)

    def add_routed(carried, group_item):
        part_grad, part_ids = group_item
        one_hot = (row_iota[:, None] == part_ids[None, :]).astype(jnp.bfloat16)
        return (carried + jnp.dot(one_hot, part_grad, preferred_element_type=jnp.float32), None)

    start_grad = jnp.zeros((owned_rows, slice_width), jnp.float32)
    row_grad, _ = lax.scan(add_routed, start_grad, (grouped_grad, grouped_ids))
    moment_one_new = 0.9 * moment_one + 0.1 * row_grad
    moment_two_new = 0.999 * moment_two + 0.001 * row_grad * row_grad
    first_fix = 1.0 - 0.9**10
    second_fix = 1.0 - 0.999**10
    update = (
        moment_one_new / first_fix / (jnp.sqrt(moment_two_new / second_fix) + 1e-08) + 0.1 * master
    )
    master_new = master - 0.05 * update
    table_slice = lax.all_gather(master_new.astype(jnp.bfloat16), "rows", axis=0, tiled=True)
    looked_up = jnp.take(table_slice, group_ids, axis=0)
    new_rows = lax.all_to_all(looked_up, "dp", split_axis=0, concat_axis=2, tiled=True)
    return (master_new, moment_one_new, moment_two_new, new_rows)


def solution(mesh):
    return jax.shard_map(
        per_device,
        mesh=mesh,
        in_specs=(
            P(("dp", "rows"), None),
            P(("dp", "rows"), None, None),
            P(("dp", "rows"), None, None),
            P(),
            P("rows", "dp"),
            P("rows", "dp"),
            P("rows", "dp"),
        ),
        out_specs=(
            P("rows", "dp"),
            P("rows", "dp"),
            P("rows", "dp"),
            P(("dp", "rows"), None, None),
        ),
        check_vma=False,
    )
```

profile of v0, /device:TPU:0, one launch (start us, length us, event | category | flops | bytes accessed | tf_op | source)
XLA Modules:
  0.0 257.8 jit_solution(5892716506937247707)
XLA Ops:
  7.2 1.8 convert_reduce_fusion
  9.0 1.9 fusion.12
  10.9 1.7 fusion.7
  12.5 2.2 fusion.4
  14.8 6.3 %copy.72 = bf16[1,128,5376]{1,0,2:T(2,128)(2,1)S(1)} copy(bf16[1,128,5376]{2,1,0:T(8,128)(2,1)} %fusion.4) | data formatting | bytes 2752512 | tf_op jit(solution)/shard_map/convert_element_type | solution.py:19
  21.0 0.5 broadcast.111
  21.6 30.3 %reduce.1 = bf16[5376,128]{1,0:T(8,128)(2,1)} reduce(bf16[5376,1,128]{2,1,0:T(2,128)(2,1)S(1)} %bitcast.47, bf16[]{:T(256)} %broadcast.111), dimensions={1}, to_apply=%bitcast.39.reduce_sub_computation | reduce | bytes 2752514
  51.8 4.1 %reshape.107 = bf16[8,2,43008]{2,1,0:T(2,128)(2,1)} reshape(bf16[5376,128]{1,0:T(8,128)(2,1)} %reduce.1) | data formatting | bytes 2752512
  56.0 7.3 %all-to-all-start.1 = ((bf16[8,2,43008]{2,1,0:T(2,128)(2,1)}), bf16[8,2,43008]{2,1,0:T(2,128)(2,1)S(1)}, u32[]{:S(2)}, u32[]{:S(2)}) async-start(bf16[8,2,43008]{2,1,0:T(2,128)(2,1)} %reshape.107), calls=%async_computation.1 | async-start | bytes 2752512 | tf_op jit(solution)/shard_map/all_to_all | solution.py:28
  63.2 37.5 %all-gather = s32[8,1,128]{2,1,0:T(1,128)S(1)} all-gather(s32[1,1,128]{2,1,0:T(1,128)S(1)} %bitcast.60), channel_id=1, replica_groups=mesh['dp'=8,'rows'=4] {'dp'}, dimensions={0}, use_global_device_ids=true | all-gather | bytes 4608 | tf_op jit(solution)/shard_map/all_gather | solution.py:26
  100.8 2.5 select_reduce_fusion.1
  103.4 0.2 select_reduce_fusion
  103.8 0.7 reshape.109
  104.5 1.1 copy-done.2
  105.5 3.4 %all-to-all-start = ((s32[4,1,256]{2,1,0:T(1,128)}), s32[4,1,256]{2,1,0:T(1,128)S(1)}, u32[]{:S(2)}, u32[]{:S(2)}) async-start(s32[4,1,256]{2,1,0:T(1,128)} %reshape.109), calls=%async_computation | async-start | bytes 8192 | tf_op jit(solution)/shard_map/all_to_all | solution.py:48
  109.0 4.5 %reshape.108 = bf16[5376,1,128]{2,1,0:T(2,128)(2,1)S(1)} reshape(bf16[8,2,43008]{2,1,0:T(2,128)(2,1)} %copy-done.2) | data formatting | bytes 2752512
  113.5 0.2 copy.79
  113.7 0.5 convolution_convert_fusion
  114.3 0.7 copy.73
  115.0 1.3 copy.74
  116.2 3.6 %all-to-all-start.2 = ((bf16[8,4,32,672]{3,2,0,1:T(8,128)(2,1)}), bf16[8,4,32,672]{3,2,0,1:T(8,128)(2,1)S(1)}, u32[]{:S(2)}, u32[]{:S(2)}) async-start(bf16[8,4,32,672]{3,2,0,1:T(8,128)(2,1)} %copy.74), calls=%async_computation.2 | async-start | bytes 3145728 | tf_op jit(solution)/shard_map/all_to_all | solution.py:47
  119.8 0.5 broadcast.112
  120.4 0.7 reduce.2
  121.2 18.6 %all-to-all-done.2 = bf16[8,4,32,672]{3,2,0,1:T(8,128)(2,1)S(1)} async-done(((bf16[8,4,32,672]{3,2,0,1:T(8,128)(2,1)}), bf16[8,4,32,672]{3,2,0,1:T(8,128)(2,1)S(1)}, u32[]{:S(2)}, u32[]{:S(2)}) %all-to-all-start.2) | async-done | bytes 1376288 | tf_op jit(solution)/shard_map/all_to_all | solution.py:47
  139.9 1.7 copy-done.5
  141.6 7.6 %fusion.25 = (bf16[1024,672]{0,1:T(8,128)(2,1)}, f32[1024,672]{0,1:T(8,128)}, f32[1024,672]{0,1:T(8,128)}, f32[1024,672]{0,1:T(8,128)}) fusion(f32[1024,672]{0,1:T(8,128)S(1)} %copy-done.5, f32[1024,672]{0,1:T(8,128)} %param.12, f32[1024,672]{0,1:T(8,128)} %param.13, bf16[1024,672]{1,0:T(8,128)(2,1)S(1)} %bitcast.53, s32[1024]{0:T(1024)S(1)} %eq.55), kind=kOutput, calls=%fused_computation.55 | convolution fusion | flops 1421344768 | bytes 19271680 | tf_op jit(solution)/shard_map/while/body/eval_jaxpr/dot_general | solution.py:59
  149.3 43.6 %all-gather.3.cloned.1.call-done = bf16[4096,672]{0,1:T(8,128)(2,1)} async-done(((bf16[1024,672]{0,1:T(8,128)(2,1)}), bf16[4096,672]{0,1:T(8,128)(2,1)}) %all-gather.3.cloned.1.call-update) | async-done | bytes 5505040 | tf_op jit(solution)/shard_map/all_gather | solution.py:71
  192.9 8.4 %copy.76 = bf16[4096,672]{1,0:T(8,128)(2,1)} copy(bf16[4096,672]{0,1:T(8,128)(2,1)} %all-gather.3.cloned.1.call-done) | data formatting | bytes 11010048 | tf_op jit(solution)/shard_map/all_gather | solution.py:71
  201.2 8.1 %gather_fusion = bf16[1024,672]{1,0:T(8,128)(2,1)S(1)} fusion(bf16[4096,672]{1,0:T(8,128)(2,1)} %copy.76, s32[1024]{0:T(1024)S(1)} %bitcast_clamp_fusion), kind=kCustom, calls=%fused_computation | custom fusion | bytes 2756608 | tf_op jit(solution)/shard_map/jit(_take)/gather | solution.py:72
  209.3 0.9 copy.77
  210.3 39.1 %all_to_all.46 = bf16[8,128,672]{1,2,0:T(8,128)(2,1)S(1)} all-to-all(bf16[8,128,672]{1,2,0:T(8,128)(2,1)S(1)} %broadcast_select_fusion), channel_id=1, replica_groups=mesh['dp'=8,'rows'=4] {'dp'}, dimensions={0} | all-to-all | bytes 2752512 | tf_op jit(solution)/shard_map/all_to_all | solution.py:73
  249.4 1.5 copy.78
  (31 shorter events, 0.8 us)
Async XLA Ops:
  7.2 3.7 %copy-start = (bf16[1,128,5376]{2,1,0:T(8,128)(2,1)S(1)}, bf16[1,128,5376]{2,1,0:T(8,128)(2,1)}, u32[]{:S(2)}) copy-start(bf16[1,128,5376]{2,1,0:T(8,128)(2,1)} %param.9) | copy-start | bytes 4128772
  7.2 3.7 %copy-start.1 = (bf16[1,128,5376]{2,1,0:T(8,128)(2,1)S(1)}, bf16[1,128,5376]{2,1,0:T(8,128)(2,1)}, u32[]{:S(2)}) copy-start(bf16[1,128,5376]{2,1,0:T(8,128)(2,1)} %param.8) | copy-start | bytes 4128772
  7.2 5.3 %copy-start.3 = (f32[5376]{0:T(1024)S(1)}, f32[5376]{0:T(1024)}, u32[]{:S(2)}) copy-start(f32[5376]{0:T(1024)} %param.10) | copy-start | bytes 64516
  51.8 11.4 %copy-start.4 = (s32[1,128]{1,0:T(1,128)S(1)}, s32[1,128]{1,0:T(1,128)}, u32[]{:S(2)}) copy-start(s32[1,128]{1,0:T(1,128)} %param.7) | copy-start | bytes 1540
  56.0 48.5 %all-to-all-start.1 = ((bf16[8,2,43008]{2,1,0:T(2,128)(2,1)}), bf16[8,2,43008]{2,1,0:T(2,128)(2,1)S(1)}, u32[]{:S(2)}, u32[]{:S(2)}) async-start(bf16[8,2,43008]{2,1,0:T(2,128)(2,1)} %reshape.107), calls=%async_computation.1 | async-start | bytes 2752512 | tf_op jit(solution)/shard_map/all_to_all | solution.py:28
  104.5 1.1 copy-start.2
  105.5 10.7 %all-to-all-start = ((s32[4,1,256]{2,1,0:T(1,128)}), s32[4,1,256]{2,1,0:T(1,128)S(1)}, u32[]{:S(2)}, u32[]{:S(2)}) async-start(s32[4,1,256]{2,1,0:T(1,128)} %reshape.109), calls=%async_computation | async-start | bytes 8192 | tf_op jit(solution)/shard_map/all_to_all | solution.py:48
  116.2 23.6 %all-to-all-start.2 = ((bf16[8,4,32,672]{3,2,0,1:T(8,128)(2,1)}), bf16[8,4,32,672]{3,2,0,1:T(8,128)(2,1)S(1)}, u32[]{:S(2)}, u32[]{:S(2)}) async-start(bf16[8,4,32,672]{3,2,0,1:T(8,128)(2,1)} %copy.74), calls=%async_computation.2 | async-start | bytes 3145728 | tf_op jit(solution)/shard_map/all_to_all | solution.py:47
  119.8 73.1 %all-gather.3.cloned.1.call-start = ((), (), s32[]{:S(2)}) async-start(), calls=%async_computation.4 | async-start | bytes 6881280 | tf_op jit(solution)/shard_map/all_gather | solution.py:71
  139.8 1.8 copy-start.5
Sparse Core Ops, SparseCore 0:
  149.4 43.4 all-gather.2
where the time goes:
time: 259 us; the launch traced here: 258 us
  blocking collectives  76.6 us (30%)
  waiting for transfers between devices  62.2 us (24%)
  other arithmetic  41.4 us (16%)
  local copies, waits for them, and re-layouts  40.9 us (16%)
  starting transfers between devices  14.3 us (6%)
  between operations  14.2 us (5%)
  matrix products  8.17 us (3%)
    all_gather x1, waiting for transfers between devices, per_device(): lax.all_gather(master_new.astype(jnp.bfloat16), 'rows', axis=0, tiled=True)  43.6 us
    all_to_all x1, blocking collectives, per_device(): lax.all_to_all(looked_up, 'dp', split_axis=0, concat_axis=2, tiled=True)  39.1 us
    all_gather x1, blocking collectives, per_device(): group_ids = lax.all_gather(token_ids, 'dp', axis=0, tiled=True)  37.5 us
    unnamed x1, other arithmetic  30.3 us
    all_to_all x1, waiting for transfers between devices, per_device(): lax.all_to_all(buckets, 'rows', split_axis=1, concat_axis=1, tiled=True)  18.6 us
    unnamed x19, local copies, waits for them, and re-layouts  14.4 us
    gather x2, local copies, waits for them, and re-layouts, per_device(): looked_up = jnp.take(table_slice, group_ids, axis=0)  8.95 us
    all_gather x1, local copies, waits for them, and re-layouts, per_device(): lax.all_gather(master_new.astype(jnp.bfloat16), 'rows', axis=0, tiled=True)  8.35 us
  transfers between devices with their start and end apart: 4, of which 2 were waited for; matrix products, arithmetic and copies ran while one was open for 5% of the time, Pallas kernels for 0%

commit v1 on v0

v1 whole, which is shorter than its diff:
```python
import functools

import jax
import jax.numpy as jnp
from jax import lax
from jax.experimental import pallas as pl
from jax.experimental.pallas import tpu as pltpu
from jax.sharding import PartitionSpec as P

LANES = 128
F32 = jnp.float32
BF16 = jnp.bfloat16


def round_up(n, m):
    return (n + m - 1) // m * m


def dot(a, b, dims):
    return lax.dot_general(a, b, (dims, ((), ())), preferred_element_type=F32)


def swap_matrix(groups, width):
    size = groups * groups * width
    row = lax.broadcasted_iota(jnp.int32, (size, size), 0)
    col = lax.broadcasted_iota(jnp.int32, (1, size), 1)
    first = lax.div(col, groups * width)
    rest = col - first * (groups * width)
    second = lax.div(rest, width)
    target = second * (groups * width) + first * width + (rest - second * width)
    return (row == target).astype(F32).astype(BF16)


def send_kernel(
    dims, ids_ref, upstream_ref, saved_ref, gain_ref, out_ref, slots_ref, grad, turned, stacked
):
    n_dp, owners, rows_owned, capacity, base = dims
    step = pl.program_id(0)
    tile, width = upstream_ref.shape
    tokens = grad.shape[0]
    values = saved_ref[...].astype(F32)
    scaled = upstream_ref[...].astype(F32) * gain_ref[...]
    centered = values - jnp.sum(values, axis=1, keepdims=True) * (1.0 / width)
    variance = jnp.sum(centered * centered, axis=1, keepdims=True) * (1.0 / width)
    inv_std = lax.rsqrt(variance + 1e-05)
    mean_scaled = jnp.sum(scaled, axis=1, keepdims=True) * (1.0 / width)
    mean_cross = inv_std * jnp.sum(scaled * centered, axis=1, keepdims=True) * (1.0 / width)
    out = inv_std * (scaled - mean_scaled - centered * (inv_std * mean_cross))
    grad[pl.ds(pl.multiple_of(step * tile, tile), tile), :] = out.astype(BF16)

    @pl.when(step == pl.num_programs(0) - 1)
    def _():
        groups = LANES // capacity
        slots = owners * capacity
        slice_width = width // n_dp
        quarter = slice_width // groups
        block = stacked.shape[0] // (n_dp * (owners // groups))
        ids = ids_ref[...]
        owner = jnp.zeros_like(ids)
        for k in range(1, owners):
            owner = owner + (ids >= k * rows_owned).astype(jnp.int32)
        local = ids - owner * rows_owned
        down = lax.broadcasted_iota(jnp.int32, (tokens, tokens), 0)
        across = lax.broadcasted_iota(jnp.int32, (tokens, tokens), 1)
        column = lambda v: jnp.sum(
            jnp.where(down == across, jnp.broadcast_to(v.astype(F32), (tokens, tokens)), 0.0),
            axis=1,
            keepdims=True,
        )
        owner_col = column(owner)
        local_col = column(local)
        earlier = (owner.astype(F32) == owner_col) & (across < down)
        rank = jnp.sum(earlier.astype(F32), axis=1, keepdims=True)
        target = (owner_col * capacity + rank).astype(jnp.int32)
        placed = target == lax.broadcasted_iota(jnp.int32, (tokens, slots), 1)
        slot_of = placed.astype(F32).astype(BF16)
        slots_ref[...] = slot_of
        slot_id = (
            jnp.sum(jnp.where(placed, local_col + 1.0, 0.0), axis=0, keepdims=True).astype(
                jnp.int32
            )
            - 1
        )
        high = lax.shift_right_arithmetic(slot_id, base)
        low = slot_id - lax.shift_left(high, base)
        high, low = high.astype(F32), low.astype(F32)
        for k in range(width // LANES):
            turned[k * LANES : (k + 1) * LANES, :] = dot(
                grad[:, k * LANES : (k + 1) * LANES], slot_of, ((0,), (0,))
            )
        tail = block - quarter
        for q in range(owners // groups):
            lanes = slice(q * LANES, (q + 1) * LANES)
            for d in range(n_dp):
                at = (q * n_dp + d) * block
                for j in range(groups):
                    start = d * slice_width + j * quarter
                    part = turned[start : start + quarter, lanes]
                    extra = (high, low)[j][:, lanes] if j < 2 else jnp.zeros((1, LANES), F32)
                    full = jnp.concatenate(
                        [part, jnp.broadcast_to(extra, (tail, LANES))], axis=0
                    ).astype(BF16)
                    stacked[at : at + block, j * LANES : (j + 1) * LANES] = full
        swapped = dot(stacked[...], swap_matrix(groups, capacity), ((1,), (0,))).astype(BF16)
        sent = out_ref.shape[1]
        for q in range(owners // groups):
            for d in range(n_dp):
                at = (q * n_dp + d) * block
                for b in range(groups):
                    out_ref[d * owners + q * groups + b] = swapped[
                        at : at + sent, b * LANES : (b + 1) * LANES
                    ]


def update_kernel(
    dims,
    arrived_ref,
    master_hbm,
    one_hbm,
    two_hbm,
    master_out,
    one_out,
    two_out,
    out_ref,
    master,
    one,
    two,
    stacked,
    turned,
    hot,
    in_sems,
    out_sems,
):
    capacity, base = dims
    groups = LANES // capacity
    sources, sent, _ = arrived_ref.shape
    slice_width, rows_owned = master.shape
    quarter = slice_width // groups
    tiles = sources // groups
    block = stacked.shape[0] // tiles
    received = sources * capacity
    hbm_in = (master_hbm, one_hbm, two_hbm)
    hbm_out = (master_out, one_out, two_out)
    held = (master, one, two)

    pieces = in_sems.shape[1]
    height = slice_width // pieces

    def copies(sources, targets, sems):
        return [
            [
                pltpu.make_async_copy(
                    source.at[p * height : (p + 1) * height, :],
                    target.at[p * height : (p + 1) * height, :],
                    sems.at[i, p],
                )
                for i, (source, target) in enumerate(zip(sources, targets))
            ]
            for p in range(pieces)
        ]

    loads = copies(hbm_in, held, in_sems)
    stores = copies(held, hbm_out, out_sems)
    for piece in loads:
        for copy in piece:
            copy.start()
    swap = swap_matrix(groups, capacity)
    for a in range(tiles):
        for b in range(groups):
            stacked[a * block : a * block + sent, b * LANES : (b + 1) * LANES] = arrived_ref[
                a * groups + b
            ]
    swapped = dot(stacked[...], swap, ((1,), (0,)))
    down = lax.broadcasted_iota(jnp.int32, (rows_owned, LANES), 0)
    for a in range(tiles):
        lanes = slice(a * LANES, (a + 1) * LANES)
        at = a * block
        for j in range(groups):
            turned[j * block : (j + 1) * block, lanes] = swapped[
                at : at + block, j * LANES : (j + 1) * LANES
            ].astype(BF16)
        id_row = sent - 1
        high = swapped[at + id_row : at + id_row + 1, 0:LANES].astype(jnp.int32)
        low = swapped[at + id_row : at + id_row + 1, LANES : 2 * LANES].astype(jnp.int32)
        ids = lax.shift_left(high, base) + low
        hot[:, lanes] = (down == ids).astype(F32).astype(BF16)
    first_fix = 1.0 - 0.9**10
    second_fix = 1.0 - 0.999**10
    for j in range(groups):
        total = dot(turned[j * block : (j + 1) * block, :], hot[...], ((1,), (1,)))[:quarter]
        if j < pieces:
            for copy in loads[j]:
                copy.wait()
        rows = slice(j * quarter, (j + 1) * quarter)
        old = master[rows, :]
        first = 0.9 * one[rows, :] + 0.1 * total
        second = 0.999 * two[rows, :] + 0.001 * total * total
        update = first / first_fix / (jnp.sqrt(second / second_fix) + 1e-08) + 0.1 * old
        new = old - 0.05 * update
        master[rows, :] = new
        one[rows, :] = first
        two[rows, :] = second
        if j >= groups - pieces:
            for copy in stores[j - (groups - pieces)]:
                copy.start()
        looked = dot(new.astype(BF16), hot[...], ((1,), (0,))).astype(BF16)
        for a in range(tiles):
            stacked[a * block : a * block + quarter, j * LANES : (j + 1) * LANES] = looked[
                :, a * LANES : (a + 1) * LANES
            ]
    back = dot(stacked[...], swap, ((1,), (0,))).astype(BF16)
    for a in range(tiles):
        for b in range(groups):
            out_ref[a * groups + b] = back[
                a * block : a * block + quarter, b * LANES : (b + 1) * LANES
            ]
    for piece in stores:
        for copy in piece:
            copy.wait()


def place_kernel(dims, rows_ref, slots_ref, out_ref, stacked, turned):
    n_dp, owners, capacity = dims
    groups = LANES // capacity
    quarter = rows_ref.shape[1]
    width = out_ref.shape[1]
    slice_width = width // n_dp
    block = stacked.shape[0] // (n_dp * (owners // groups))
    for q in range(owners // groups):
        for d in range(n_dp):
            at = (q * n_dp + d) * block
            for b in range(groups):
                stacked[at : at + quarter, b * LANES : (b + 1) * LANES] = rows_ref[
                    d * owners + q * groups + b
                ]
    swapped = dot(stacked[...], swap_matrix(groups, capacity), ((1,), (0,)))
    for q in range(owners // groups):
        for d in range(n_dp):
            at = (q * n_dp + d) * block
            for j in range(groups):
                start = d * slice_width + j * quarter
                turned[start : start + quarter, q * LANES : (q + 1) * LANES] = swapped[
                    at : at + quarter, j * LANES : (j + 1) * LANES
                ]
    for k in range(width // LANES):
        lanes = slice(k * LANES, (k + 1) * LANES)
        out_ref[:, lanes] = dot(
            slots_ref[...], turned[lanes, :].astype(BF16), ((1,), (1,))
        ).astype(BF16)


def per_device(token_ids, upstream, saved_rows, norm_gain, master, moment_one, moment_two):
    axes = ("dp", "rows")
    n_dp, owners = lax.axis_size("dp"), lax.axis_size("rows")
    devices = n_dp * owners
    _, tokens, width = upstream.shape
    rows_owned, slice_width = master.shape
    capacity = tokens // 4
    groups = LANES // capacity
    quarter = slice_width // groups
    sent = round_up(quarter, 8) + 8
    pieces = groups if quarter % 8 == 0 else 1
    block = round_up(sent, 16)
    slots = owners * capacity
    stack = devices // groups * block
    tile = 16
    base = 7
    full = pl.BlockSpec(memory_space=pltpu.VMEM)
    hbm = pl.BlockSpec(memory_space=pl.ANY)
    blocks, slot_of = pl.pallas_call(
        functools.partial(send_kernel, (n_dp, owners, rows_owned, capacity, base)),
        grid=(tokens // tile,),
        in_specs=[
            pl.BlockSpec((1, tokens), lambda i: (0, 0)),
            pl.BlockSpec((tile, width), lambda i: (i, 0)),
            pl.BlockSpec((tile, width), lambda i: (i, 0)),
            pl.BlockSpec((1, width), lambda i: (0, 0)),
        ],
        out_specs=[
            pl.BlockSpec((devices, sent, LANES), lambda i: (0, 0, 0)),
            pl.BlockSpec((tokens, slots), lambda i: (0, 0)),
        ],
        out_shape=[
            jax.ShapeDtypeStruct((devices, sent, LANES), BF16),
            jax.ShapeDtypeStruct((tokens, slots), BF16),
        ],
        scratch_shapes=[
            pltpu.VMEM((tokens, width), BF16),
            pltpu.VMEM((width, slots), F32),
            pltpu.VMEM((stack, groups * LANES), BF16),
        ],
        name="send",
    )(token_ids, upstream[0], saved_rows[0], norm_gain[None])
    arrived = lax.all_to_all(blocks, axes, split_axis=0, concat_axis=0, tiled=True)
    state = jax.ShapeDtypeStruct((slice_width, rows_owned), F32)
    master_new, one_new, two_new, found = pl.pallas_call(
        functools.partial(update_kernel, (capacity, base)),
        in_specs=[full, hbm, hbm, hbm],
        out_specs=[hbm, hbm, hbm, full],
        out_shape=[state, state, state, jax.ShapeDtypeStruct((devices, quarter, LANES), BF16)],
        scratch_shapes=[
            pltpu.VMEM(state.shape, F32),
            pltpu.VMEM(state.shape, F32),
            pltpu.VMEM(state.shape, F32),
            pltpu.VMEM((stack, groups * LANES), BF16),
            pltpu.VMEM((groups * block, devices * capacity), BF16),
            pltpu.VMEM((rows_owned, devices * capacity), BF16),
            pltpu.SemaphoreType.DMA((3, pieces)),
            pltpu.SemaphoreType.DMA((3, pieces)),
        ],
        name="update",
    )(arrived, master.T, moment_one.T, moment_two.T)
    rows = lax.all_to_all(found, axes, split_axis=0, concat_axis=0, tiled=True)
    new_rows = pl.pallas_call(
        functools.partial(place_kernel, (n_dp, owners, capacity)),
        in_specs=[full, full],
        out_specs=full,
        out_shape=jax.ShapeDtypeStruct((tokens, width), BF16),
        scratch_shapes=[
            pltpu.VMEM((stack, groups * LANES), BF16),
            pltpu.VMEM((width, slots), F32),
        ],
        name="place",
    )(rows, slot_of)
    return (master_new.T, one_new.T, two_new.T, new_rows[None])


def solution(mesh):
    split = P(("dp", "rows"), None, None)
    slab = P("rows", "dp")
    return jax.shard_map(
        per_device,
        mesh=mesh,
        in_specs=(P(("dp", "rows"), None), split, split, P(), slab, slab, slab),
        out_specs=(slab, slab, slab, split),
        check_vma=False,
    )
```

time: 259 us -> 108 us (0.42)
  waiting for transfers between devices: 62.2 us -> 0 us
  other arithmetic: 41.4 us -> 0 us
  local copies, waits for them, and re-layouts: 40.9 us -> 1.36 us
  Pallas kernels: 0 us -> 24.3 us
  starting transfers between devices: 14.3 us -> 0 us
  between operations: 14.2 us -> 0.64 us
  matrix products: 8.17 us -> 0 us
  blocking collectives: 76.6 us -> 81.1 us
    all_gather x1 -> x0, waiting for transfers between devices: 43.6 us -> none  [per_device(): lax.all_gather(master_new.astype(jnp.bfloat16), 'rows', axis=0, tiled=True)]
    all_to_all x1 -> x2, blocking collectives: 39.1 us -> 81.1 us  [the longest x1 43.2 us: per_device(): lax.all_to_all(blocks, axes, split_axis=0, concat_axis=0, tiled=True)]
    all_gather x1 -> x0, blocking collectives: 37.5 us -> none  [per_device(): group_ids = lax.all_gather(token_ids, 'dp', axis=0, tiled=True)]
    unnamed x1 -> x0, other arithmetic: 30.3 us -> none
    pallas_call x0 -> x3, Pallas kernels: none -> 24.3 us  [the longest x1 11.4 us: per_device(): pl.pallas_call(functools.partial(update_kernel, (capacity, base)), in_spe...]
    all_to_all x3 -> x0, waiting for transfers between devices: 18.6 us -> none  [the longest x1 18.6 us: per_device(): lax.all_to_all(buckets, 'rows', split_axis=1, concat_axis=1, tiled=True)]
    unnamed x19 -> x0, local copies, waits for them, and re-layouts: 14.4 us -> none
    all_to_all x3 -> x0, starting transfers between devices: 14.3 us -> none  [the longest x1 7.28 us: per_device(): lax.all_to_all(row_input, 'dp', split_axis=2, concat_axis=0, tiled=True)]
  transfers between devices with their start and end apart: 4 -> 0, of which waited for: 2 -> 0; matrix products, arithmetic and copies ran while one was open for 5% -> 0% of each run, Pallas kernels for 0% -> 0%
where the time goes in v1:
time: 108 us; the launch traced here: 107 us
  blocking collectives  81.1 us (75%)
  Pallas kernels  24.3 us (22%)
  local copies, waits for them, and re-layouts  1.36 us (1%)
    all_to_all x1, blocking collectives, per_device(): lax.all_to_all(blocks, axes, split_axis=0, concat_axis=0, tiled=True)  43.2 us
    all_to_all x1, blocking collectives, per_device(): rows = lax.all_to_all(found, axes, split_axis=0, concat_axis=0, tiled=True)  37.9 us
    pallas_call x1, Pallas kernels, per_device(): pl.pallas_call(functools.partial(update_kernel, (capacity, base)), in_spe...  11.4 us
    pallas_call x1, Pallas kernels, per_device(): pl.pallas_call(functools.partial(send_kernel, (n_dp, owners, rows_owned,...  8.59 us
    pallas_call x1, Pallas kernels, per_device(): pl.pallas_call(functools.partial(place_kernel, (n_dp, owners, capacity)),...  4.29 us

profile of v1, /device:TPU:0, one launch (start us, length us, event | category | flops | bytes accessed | tf_op | source)
XLA Modules:
  0.0 107.3 jit_solution(1241847072195294016)
XLA Ops:
  0.6 1.4 %broadcast_in_dim.6.gain_ref = f32[1,5376]{1,0:T(1,128)} reshape(f32[5376]{0:T(1024)} %param.10) | data formatting | bytes 43008 | tf_op jit(solution)/shard_map/broadcast_in_dim | solution.py:293
  2.0 8.6 %send.1 = (bf16[32,176,128]{2,1,0:T(8,128)(2,1)}, bf16[128,128]{1,0:T(8,128)(2,1)}) custom-call(s32[1,128]{1,0:T(1,128)} %ids_ref.1, bf16[128,5376]{1,0:T(8,128)(2,1)} %bitcast.12, bf16[128,5376]{1,0:T(8,128)(2,1)} %bitcast.13, f32[1,5376]{1,0:T(1,128)} %broadcast_in_dim.6.gain_ref), custom_call_target="tpu_custom_call" | custom-call | tf_op jit(solution)/shard_map/send/pallas_call | solution.py:270
  10.6 43.2 %all_to_all.10.arrived_ref = bf16[32,176,128]{2,1,0:T(8,128)(2,1)} all-to-all(bf16[32,176,128]{2,1,0:T(8,128)(2,1)} %get-tuple-element.10), channel_id=1, replica_groups=mesh['dp'=8,'rows'=4] {'dp','rows'}, dimensions={0} | all-to-all | bytes 2883584 | tf_op jit(solution)/shard_map/all_to_all | solution.py:294
  53.7 11.4 %update.1 = (f32[672,1024]{1,0:T(8,128)}, f32[672,1024]{1,0:T(8,128)}, f32[672,1024]{1,0:T(8,128)}, bf16[32,168,128]{2,1,0:T(8,128)(2,1)}) custom-call(bf16[32,176,128]{2,1,0:T(8,128)(2,1)} %all_to_all.10.arrived_ref, f32[672,1024]{1,0:T(8,128)} %bitcast.9, f32[672,1024]{1,0:T(8,128)} %bitcast.10, f32[672,1024]{1,0:T(8,128)} %bitcast.11), custom_call_target="tpu_custom_call" | custom-call | tf_op jit(solution)/shard_map/update/pallas_call | solution.py:296
  65.1 37.9 %all_to_all.11.rows_ref = bf16[32,168,128]{2,1,0:T(8,128)(2,1)} all-to-all(bf16[32,168,128]{2,1,0:T(8,128)(2,1)} %get-tuple-element.14), channel_id=1, replica_groups=mesh['dp'=8,'rows'=4] {'dp','rows'}, dimensions={0} | all-to-all | bytes 2752512 | tf_op jit(solution)/shard_map/all_to_all | solution.py:313
  103.0 4.3 %place.1 = bf16[128,5376]{1,0:T(8,128)(2,1)} custom-call(bf16[32,168,128]{2,1,0:T(8,128)(2,1)} %all_to_all.11.rows_ref, bf16[128,128]{1,0:T(8,128)(2,1)} %get-tuple-element.15.slots_ref), custom_call_target="tpu_custom_call" | custom-call | tf_op jit(solution)/shard_map/place/pallas_call | solution.py:314

commit v2 on v1

v2 whole, which is shorter than its diff:
```python
import functools

import jax
import jax.numpy as jnp
from jax import lax
from jax.experimental import pallas as pl
from jax.experimental.pallas import tpu as pltpu
from jax.sharding import PartitionSpec as P

LANES = 128
F32 = jnp.float32
BF16 = jnp.bfloat16


def round_up(n, m):
    return (n + m - 1) // m * m


def dot(a, b, dims):
    return lax.dot_general(a, b, (dims, ((), ())), preferred_element_type=F32)


def swap_matrix(groups, width):
    size = groups * groups * width
    row = lax.broadcasted_iota(jnp.int32, (size, size), 0)
    col = lax.broadcasted_iota(jnp.int32, (1, size), 1)
    first = lax.div(col, groups * width)
    rest = col - first * (groups * width)
    second = lax.div(rest, width)
    target = second * (groups * width) + first * width + (rest - second * width)
    return (row == target).astype(F32).astype(BF16)


def send_kernel(
    dims,
    ids_hbm,
    upstream_hbm,
    saved_hbm,
    gain_hbm,
    out_ref,
    slots_ref,
    ids_ref,
    gain_ref,
    upstream,
    saved,
    values,
    scaled,
    stats,
    turned,
    stacked,
    sems,
    small_sems,
):
    n_dp, owners, rows_owned, capacity, base = dims
    tokens, width = values.shape
    tile = tokens // sems.shape[1]
    columns = [slice(k * LANES, (k + 1) * LANES) for k in range(width // LANES)]
    zero = jnp.zeros((tile, LANES), F32)

    def part(step):
        return pl.ds(pl.multiple_of(step * tile, tile), tile)

    def copies(step):
        return (
            pltpu.make_async_copy(saved_hbm.at[part(step)], saved.at[part(step)], sems.at[0, step]),
            pltpu.make_async_copy(
                upstream_hbm.at[part(step)], upstream.at[part(step)], sems.at[1, step]
            ),
        )

    gain_copy = pltpu.make_async_copy(gain_hbm, gain_ref, small_sems.at[0])
    ids_copy = pltpu.make_async_copy(ids_hbm, ids_ref, small_sems.at[1])
    gain_copy.start()
    for step in range(tokens // tile):
        for copy in copies(step):
            copy.start()
        if step == 0:
            ids_copy.start()
    gain_copy.wait()

    def mean(partial):
        return jnp.sum(partial, axis=1, keepdims=True) * (1.0 / width)

    @pl.loop(0, tokens // tile)
    def _(step):
        for copy in copies(step):
            copy.wait()
        here = part(step)
        sum_value, sum_scaled = zero, zero
        for k, lanes in enumerate(columns):
            value = saved[here, lanes].astype(F32)
            scale = upstream[here, lanes].astype(F32) * gain_ref[k : k + 1, :]
            values[here, lanes] = value
            scaled[here, lanes] = scale
            sum_value += value
            sum_scaled += scale
        row_mean = jnp.broadcast_to(mean(sum_value), (tile, LANES))
        square, cross = zero, zero
        for lanes in columns:
            centered = values[here, lanes] - row_mean
            square += centered * centered
            cross += centered * scaled[here, lanes]
        inv_std = lax.rsqrt(mean(square) + 1e-05)
        along = inv_std * inv_std * inv_std * mean(cross)
        shift = inv_std * mean(sum_scaled)
        for i, stat in enumerate((row_mean, inv_std, along, shift)):
            stats[i, here, :] = jnp.broadcast_to(stat, (tile, LANES))

    row_mean, inv_std, along, shift = (stats[i] for i in range(4))
    ids_copy.wait()
    groups = LANES // capacity
    slots = owners * capacity
    slice_width = width // n_dp
    quarter = slice_width // groups
    block = stacked.shape[0] // (n_dp * (owners // groups))
    ids = ids_ref[...]
    owner = jnp.zeros_like(ids)
    for k in range(1, owners):
        owner = owner + (ids >= k * rows_owned).astype(jnp.int32)
    local = ids - owner * rows_owned
    down = lax.broadcasted_iota(jnp.int32, (tokens, tokens), 0)
    across = lax.broadcasted_iota(jnp.int32, (tokens, tokens), 1)
    column = lambda v: jnp.sum(
        jnp.where(down == across, jnp.broadcast_to(v.astype(F32), (tokens, tokens)), 0.0),
        axis=1,
        keepdims=True,
    )
    owner_col = column(owner)
    local_col = column(local)
    earlier = (owner.astype(F32) == owner_col) & (across < down)
    rank = jnp.sum(earlier.astype(F32), axis=1, keepdims=True)
    target = (owner_col * capacity + rank).astype(jnp.int32)
    placed = target == lax.broadcasted_iota(jnp.int32, (tokens, slots), 1)
    slot_of = placed.astype(F32).astype(BF16)
    slots_ref[...] = slot_of
    slot_id = (
        jnp.sum(jnp.where(placed, local_col + 1.0, 0.0), axis=0, keepdims=True).astype(
            jnp.int32
        )
        - 1
    )
    high = lax.shift_right_arithmetic(slot_id, base)
    low = slot_id - lax.shift_left(high, base)
    high, low = high.astype(F32), low.astype(F32)
    for lanes in columns:
        grad = inv_std * scaled[:, lanes] - shift - along * (values[:, lanes] - row_mean)
        turned[lanes, :] = dot(grad.astype(BF16), slot_of, ((0,), (0,)))
    tail = block - quarter
    for q in range(owners // groups):
        lanes = slice(q * LANES, (q + 1) * LANES)
        for d in range(n_dp):
            at = (q * n_dp + d) * block
            for j in range(groups):
                start = d * slice_width + j * quarter
                part = turned[start : start + quarter, lanes]
                extra = (high, low)[j][:, lanes] if j < 2 else jnp.zeros((1, LANES), F32)
                full = jnp.concatenate(
                    [part, jnp.broadcast_to(extra, (tail, LANES))], axis=0
                ).astype(BF16)
                stacked[at : at + block, j * LANES : (j + 1) * LANES] = full
    swapped = dot(stacked[...], swap_matrix(groups, capacity), ((1,), (0,))).astype(BF16)
    sent = out_ref.shape[1]
    for q in range(owners // groups):
        for d in range(n_dp):
            at = (q * n_dp + d) * block
            for b in range(groups):
                out_ref[d * owners + q * groups + b] = swapped[
                    at : at + sent, b * LANES : (b + 1) * LANES
                ]


def adam(old, first, second):
    fixed = second * (1.0 / (1.0 - 0.999**10))
    scale = fixed * lax.rsqrt(fixed) + 1e-08
    return old - (0.05 / (1.0 - 0.9**10)) * first / scale


def update_kernel(
    dims,
    arrived_ref,
    master,
    one,
    old_two_hbm,
    out_ref,
    master_hbm,
    one_hbm,
    two_hbm,
    total,
    stacked,
    turned,
    hot,
    table,
    two,
    master_new,
    one_new,
    two_new,
    sems,
    load_sem,
):
    capacity, base = dims
    groups = LANES // capacity
    sources, sent, _ = arrived_ref.shape
    slice_width, rows_owned = master.shape
    quarter = slice_width // groups
    tiles = sources // groups
    block = stacked.shape[0] // tiles
    span = 2 * LANES
    load = pltpu.make_async_copy(old_two_hbm, two, load_sem)
    load.start()
    swap = swap_matrix(groups, capacity)
    for a in range(tiles):
        for b in range(groups):
            stacked[a * block : a * block + sent, b * LANES : (b + 1) * LANES] = arrived_ref[
                a * groups + b
            ]
    down = lax.broadcasted_iota(jnp.int16, (rows_owned, LANES), 0)
    one_of, none_of = jnp.ones((rows_owned, LANES), BF16), jnp.zeros((rows_owned, LANES), BF16)
    id_row = sent - 1
    for a in range(tiles):
        lanes = slice(a * LANES, (a + 1) * LANES)
        swapped = dot(stacked[a * block : (a + 1) * block, :], swap, ((1,), (0,)))
        for j in range(groups):
            turned[j * block : (j + 1) * block, lanes] = swapped[
                :, j * LANES : (j + 1) * LANES
            ].astype(BF16)
        high = swapped[id_row : id_row + 1, 0:LANES].astype(jnp.int32)
        low = swapped[id_row : id_row + 1, LANES : 2 * LANES].astype(jnp.int32)
        ids = (lax.shift_left(high, base) + low).astype(jnp.int16)
        hot[:, lanes] = jnp.where(down == ids, one_of, none_of)

    def gather_rows(j, n):
        lanes = slice(n * span, (n + 1) * span)
        total[j * block : (j + 1) * block, lanes] = dot(
            turned[j * block : (j + 1) * block, :], hot[lanes, :], ((1,), (1,))
        )

    def step_rows(j, lanes):
        for top in range(0, quarter, 16):
            size = min(16, quarter - top)
            rows = slice(j * quarter + top, j * quarter + top + size)
            grad = total[j * block + top : j * block + top + size, lanes]
            first = 0.9 * one[rows, lanes] + 0.1 * grad
            second = 0.999 * two[rows, lanes] + 0.001 * grad * grad
            new = adam(0.995 * master[rows, lanes], first, second)
            one_new[rows, lanes] = first
            two_new[rows, lanes] = second
            master_new[rows, lanes] = new
            if size < 16:
                new = jnp.concatenate([new, jnp.zeros((16 - size, LANES), F32)], axis=0)
            table[j * block + top : j * block + top + 16, lanes] = new.astype(BF16)

    def look_rows(j, n):
        looked = dot(
            table[j * block : (j + 1) * block, :],
            hot[:, n * span : (n + 1) * span],
            ((1,), (0,)),
        ).astype(BF16)
        for h in range(2):
            at = (2 * n + h) * block
            stacked[at : at + block, j * LANES : (j + 1) * LANES] = looked[
                :, h * LANES : (h + 1) * LANES
            ]

    pieces = sems.shape[1]
    height = slice_width // pieces
    stores = [
        [
            pltpu.make_async_copy(
                held.at[p * height : (p + 1) * height], hbm.at[p * height : (p + 1) * height], sems.at[i, p]
            )
            for i, (held, hbm) in enumerate(
                ((master_new, master_hbm), (one_new, one_hbm), (two_new, two_hbm))
            )
        ]
        for p in range(pieces)
    ]
    load.wait()
    for n in range(rows_owned // span):
        gather_rows(0, n)
    for j in range(groups + 1):
        for n in range(max(rows_owned // span, tiles // 2)):
            if j + 1 < groups and n < rows_owned // span:
                gather_rows(j + 1, n)
            if j > 0 and n < tiles // 2:
                look_rows(j - 1, n)
            if j < groups and n < rows_owned // span:
                for h in range(2):
                    step_rows(j, slice((2 * n + h) * LANES, (2 * n + h + 1) * LANES))
        if groups - pieces <= j < groups:
            for copy in stores[j - groups + pieces]:
                copy.start()
    for a in range(tiles):
        back = dot(stacked[a * block : (a + 1) * block, :], swap, ((1,), (0,))).astype(BF16)
        for b in range(groups):
            out_ref[a * groups + b] = back[:quarter, b * LANES : (b + 1) * LANES]
    for piece in stores:
        for copy in piece:
            copy.wait()


def place_kernel(dims, rows_ref, slots_ref, out_ref, stacked, turned):
    n_dp, owners, capacity = dims
    groups = LANES // capacity
    quarter = rows_ref.shape[1]
    width = out_ref.shape[1]
    slice_width = width // n_dp
    block = stacked.shape[0] // (n_dp * (owners // groups))
    for q in range(owners // groups):
        for d in range(n_dp):
            at = (q * n_dp + d) * block
            for b in range(groups):
                stacked[at : at + quarter, b * LANES : (b + 1) * LANES] = rows_ref[
                    d * owners + q * groups + b
                ]
    swapped = dot(stacked[...], swap_matrix(groups, capacity), ((1,), (0,)))
    for q in range(owners // groups):
        for d in range(n_dp):
            at = (q * n_dp + d) * block
            for j in range(groups):
                start = d * slice_width + j * quarter
                turned[start : start + quarter, q * LANES : (q + 1) * LANES] = swapped[
                    at : at + quarter, j * LANES : (j + 1) * LANES
                ]
    for k in range(0, width, 2 * LANES):
        lanes = slice(k, min(k + 2 * LANES, width))
        out_ref[:, lanes] = dot(
            slots_ref[...], turned[lanes, :].astype(BF16), ((1,), (1,))
        ).astype(BF16)


def per_device(token_ids, upstream, saved_rows, norm_gain, master, moment_one, moment_two):
    axes = ("dp", "rows")
    n_dp, owners = lax.axis_size("dp"), lax.axis_size("rows")
    devices = n_dp * owners
    _, tokens, width = upstream.shape
    rows_owned, slice_width = master.shape
    capacity = tokens // 4
    groups = LANES // capacity
    quarter = slice_width // groups
    sent = round_up(quarter, 8) + 8
    block = round_up(sent, 16)
    slots = owners * capacity
    stack = devices // groups * block
    tile = 16
    base = 7
    full = pl.BlockSpec(memory_space=pltpu.VMEM)

    def params(mib):
        if devices * capacity > rows_owned:
            mib = 60
        return pltpu.CompilerParams(vmem_limit_bytes=mib * 2**20)

    hbm = pl.BlockSpec(memory_space=pltpu.HBM)
    blocks, slot_of = pl.pallas_call(
        functools.partial(send_kernel, (n_dp, owners, rows_owned, capacity, base)),
        in_specs=[hbm] * 4,
        out_specs=[full] * 2,
        out_shape=[
            jax.ShapeDtypeStruct((devices, sent, LANES), BF16),
            jax.ShapeDtypeStruct((tokens, slots), BF16),
        ],
        scratch_shapes=[
            pltpu.VMEM((1, tokens), jnp.int32),
            pltpu.VMEM((width // LANES, LANES), F32),
            pltpu.VMEM((tokens, width), BF16),
            pltpu.VMEM((tokens, width), BF16),
            pltpu.VMEM((tokens, width), F32),
            pltpu.VMEM((tokens, width), F32),
            pltpu.VMEM((4, tokens, LANES), F32),
            pltpu.VMEM((width, slots), F32),
            pltpu.VMEM((stack, groups * LANES), BF16),
            pltpu.SemaphoreType.DMA((2, tokens // tile)),
            pltpu.SemaphoreType.DMA((2,)),
        ],
        compiler_params=params(20),
        name="send",
    )(
        *(
            pltpu.with_memory_space_constraint(x, pltpu.HBM)
            for x in (
                token_ids,
                upstream[0],
                saved_rows[0],
                norm_gain.reshape(width // LANES, LANES),
            )
        )
    )
    arrived = lax.all_to_all(blocks, axes, split_axis=0, concat_axis=0, tiled=True)
    state = jax.ShapeDtypeStruct((slice_width, rows_owned), F32)
    slab = (master.T, moment_one.T, moment_two.T)
    found, master_new, one_new, two_new = pl.pallas_call(
        functools.partial(update_kernel, (capacity, base)),
        in_specs=[full] * 3 + [hbm],
        out_specs=[full] + [hbm] * 3,
        out_shape=[jax.ShapeDtypeStruct((devices, quarter, LANES), BF16)] + [state] * 3,
        scratch_shapes=[
            pltpu.VMEM((groups * block, rows_owned), F32),
            pltpu.VMEM((stack, groups * LANES), BF16),
            pltpu.VMEM((groups * block, devices * capacity), BF16),
            pltpu.VMEM((rows_owned, devices * capacity), BF16),
            pltpu.VMEM((groups * block, rows_owned), BF16),
            pltpu.VMEM(state.shape, F32),
            pltpu.VMEM(state.shape, F32),
            pltpu.VMEM(state.shape, F32),
            pltpu.VMEM(state.shape, F32),
            pltpu.SemaphoreType.DMA((3, groups if quarter % 8 == 0 else 1)),
            pltpu.SemaphoreType.DMA,
        ],
        compiler_params=params(28),
        name="update",
    )(arrived, slab[0], slab[1], pltpu.with_memory_space_constraint(slab[2], pltpu.HBM))
    rows = lax.all_to_all(found, axes, split_axis=0, concat_axis=0, tiled=True)
    new_rows = pl.pallas_call(
        functools.partial(place_kernel, (n_dp, owners, capacity)),
        in_specs=[full, full],
        out_specs=full,
        out_shape=jax.ShapeDtypeStruct((tokens, width), BF16),
        scratch_shapes=[
            pltpu.VMEM((stack, groups * LANES), BF16),
            pltpu.VMEM((width, slots), F32),
        ],
        compiler_params=params(16),
        name="place",
    )(rows, slot_of)
    return (master_new.T, one_new.T, two_new.T, new_rows[None])


def solution(mesh):
    split = P(("dp", "rows"), None, None)
    slab = P("rows", "dp")
    return jax.shard_map(
        per_device,
        mesh=mesh,
        in_specs=(P(("dp", "rows"), None), split, split, P(), slab, slab, slab),
        out_specs=(slab, slab, slab, split),
        check_vma=False,
    )
```

time: 108 us -> 98.1 us (0.908)
  Pallas kernels: 24.3 us -> 17.5 us
  blocking collectives: 81.1 us -> 79.7 us
  local copies, waits for them, and re-layouts: 1.36 us -> 0.01 us
    pallas_call x1, Pallas kernels: 8.59 us -> 5.97 us  [per_device(): pl.pallas_call(functools.partial(send_kernel, (n_dp, owners, rows_owned,...]
    pallas_call x1, Pallas kernels: 11.4 us -> 9.15 us  [per_device(): pl.pallas_call(functools.partial(update_kernel, (capacity, base)), in_spe...]
    pallas_call x1, Pallas kernels: 4.29 us -> 2.39 us  [per_device(): pl.pallas_call(functools.partial(place_kernel, (n_dp, owners, capacity)),...]
    broadcast_in_dim x1 -> x0, local copies, waits for them, and re-layouts: 1.36 us -> none  [per_device(): norm_gain[None]]
where the time goes in v2:
time: 98.1 us; the launch traced here: 97.9 us
  blocking collectives  79.7 us (81%)
  Pallas kernels  17.5 us (18%)
    all_to_all x1, blocking collectives, per_device(): lax.all_to_all(blocks, axes, split_axis=0, concat_axis=0, tiled=True)  42.8 us
    all_to_all x1, blocking collectives, per_device(): rows = lax.all_to_all(found, axes, split_axis=0, concat_axis=0, tiled=True)  36.9 us
    pallas_call x1, Pallas kernels, per_device(): pl.pallas_call(functools.partial(update_kernel, (capacity, base)), in_spe...  9.15 us
    pallas_call x1, Pallas kernels, per_device(): pl.pallas_call(functools.partial(send_kernel, (n_dp, owners, rows_owned,...  5.97 us
    pallas_call x1, Pallas kernels, per_device(): pl.pallas_call(functools.partial(place_kernel, (n_dp, owners, capacity)),...  2.39 us

profile of v2, /device:TPU:0, one launch (start us, length us, event | category | flops | bytes accessed | tf_op | source)
XLA Modules:
  0.0 97.9 jit_solution(15015451416730462289)
XLA Ops:
  0.6 0.0 copy-start.1
  0.6 6.0 %send.1 = (bf16[32,176,128]{2,1,0:T(8,128)(2,1)S(1)}, bf16[128,128]{1,0:T(8,128)(2,1)S(1)}) custom-call(s32[1,128]{1,0:T(1,128)} %ids_hbm.1, bf16[128,5376]{1,0:T(8,128)(2,1)} %bitcast.13, bf16[128,5376]{1,0:T(8,128)(2,1)} %bitcast.14, f32[42,128]{1,0:T(8,128)} %bitcast.16), custom_call_target="tpu_custom_call" | custom-call | tf_op jit(solution)/shard_map/send/pallas_call | solution.py:354
  6.6 0.0 copy-start
  6.6 42.8 %all_to_all.10.arrived_ref = bf16[32,176,128]{2,1,0:T(8,128)(2,1)S(1)} all-to-all(bf16[32,176,128]{2,1,0:T(8,128)(2,1)S(1)} %get-tuple-element.10), channel_id=1, replica_groups=mesh['dp'=8,'rows'=4] {'dp','rows'}, dimensions={0} | all-to-all | bytes 2883584 | tf_op jit(solution)/shard_map/all_to_all | solution.py:388
  49.5 0.0 copy-done.1
  49.5 0.0 copy-done
  49.5 9.2 %update.1 = (bf16[32,168,128]{2,1,0:T(8,128)(2,1)S(1)}, f32[672,1024]{1,0:T(8,128)}, f32[672,1024]{1,0:T(8,128)}, f32[672,1024]{1,0:T(8,128)}) custom-call(bf16[32,176,128]{2,1,0:T(8,128)(2,1)S(1)} %all_to_all.10.arrived_ref, f32[672,1024]{1,0:T(8,128)S(1)} %bitcast.10, f32[672,1024]{1,0:T(8,128)S(1)} %bitcast.11, f32[672,1024]{1,0:T(8,128)} %bitcast.12), custom_call_target="tpu_custom_call" | custom-call | tf_op jit(solution)/shard_map/update/pallas_call | solution.py:391
  58.6 36.9 %all_to_all.11.rows_ref = bf16[32,168,128]{2,1,0:T(8,128)(2,1)S(1)} all-to-all(bf16[32,168,128]{2,1,0:T(8,128)(2,1)S(1)} %get-tuple-element.14), channel_id=1, replica_groups=mesh['dp'=8,'rows'=4] {'dp','rows'}, dimensions={0} | all-to-all | bytes 2752512 | tf_op jit(solution)/shard_map/all_to_all | solution.py:412
  95.5 2.4 %place.1 = bf16[128,5376]{1,0:T(8,128)(2,1)} custom-call(bf16[32,168,128]{2,1,0:T(8,128)(2,1)S(1)} %all_to_all.11.rows_ref, bf16[128,128]{1,0:T(8,128)(2,1)S(1)} %get-tuple-element.15.slots_ref), custom_call_target="tpu_custom_call" | custom-call | tf_op jit(solution)/shard_map/place/pallas_call | solution.py:413
Async XLA Ops:
  0.6 48.9 %copy-start.1 = (f32[1024,672]{0,1:T(8,128)S(1)}, f32[1024,672]{0,1:T(8,128)}, u32[]{:S(2)}) copy-start(f32[1024,672]{0,1:T(8,128)} %param.12) | copy-start | bytes 8257540
  6.6 42.9 %copy-start = (f32[1024,672]{0,1:T(8,128)S(1)}, f32[1024,672]{0,1:T(8,128)}, u32[]{:S(2)}) copy-start(f32[1024,672]{0,1:T(8,128)} %param.11) | copy-start | bytes 8257540

commit v3 on v2

--- a/solution.py
+++ b/solution.py
@@ -102,11 +102,10 @@
             cross += centered * scaled[here, lanes]
         inv_std = lax.rsqrt(mean(square) + 1e-05)
         along = inv_std * inv_std * inv_std * mean(cross)
-        shift = inv_std * mean(sum_scaled)
-        for i, stat in enumerate((row_mean, inv_std, along, shift)):
+        shift = along * row_mean - inv_std * mean(sum_scaled)
+        for i, stat in enumerate((inv_std, along, shift)):
             stats[i, here, :] = jnp.broadcast_to(stat, (tile, LANES))
 
-    row_mean, inv_std, along, shift = (stats[i] for i in range(4))
     ids_copy.wait()
     groups = LANES // capacity
     slots = owners * capacity
@@ -142,37 +141,51 @@
     high = lax.shift_right_arithmetic(slot_id, base)
     low = slot_id - lax.shift_left(high, base)
     high, low = high.astype(F32), low.astype(F32)
-    for lanes in columns:
-        grad = inv_std * scaled[:, lanes] - shift - along * (values[:, lanes] - row_mean)
-        turned[lanes, :] = dot(grad.astype(BF16), slot_of, ((0,), (0,)))
     tail = block - quarter
-    for q in range(owners // groups):
-        lanes = slice(q * LANES, (q + 1) * LANES)
-        for d in range(n_dp):
-            at = (q * n_dp + d) * block
-            for j in range(groups):
-                start = d * slice_width + j * quarter
-                part = turned[start : start + quarter, lanes]
-                extra = (high, low)[j][:, lanes] if j < 2 else jnp.zeros((1, LANES), F32)
-                full = jnp.concatenate(
-                    [part, jnp.broadcast_to(extra, (tail, LANES))], axis=0
-                ).astype(BF16)
-                stacked[at : at + block, j * LANES : (j + 1) * LANES] = full
-    swapped = dot(stacked[...], swap_matrix(groups, capacity), ((1,), (0,))).astype(BF16)
     sent = out_ref.shape[1]
-    for q in range(owners // groups):
-        for d in range(n_dp):
-            at = (q * n_dp + d) * block
-            for b in range(groups):
-                out_ref[d * owners + q * groups + b] = swapped[
-                    at : at + sent, b * LANES : (b + 1) * LANES
-                ]
+    swap = swap_matrix(groups, capacity)
+    ready, chunk = 0, 4
+    for first in range(0, n_dp, chunk):
+        while ready * LANES < (first + chunk) * slice_width:
+            lanes = columns[ready]
+            grad = stats[0] * scaled[:, lanes] - stats[1] * values[:, lanes] + stats[2]
+            turned[lanes, :] = dot(grad.astype(BF16), slot_of, ((0,), (0,)))
+            ready += 1
+        for q in range(owners // groups):
+            lanes = slice(q * LANES, (q + 1) * LANES)
+            base_at = (q * n_dp + first) * block
+            for d in range(chunk):
+                at = base_at + d * block
+                for j in range(groups):
+                    start = (first + d) * slice_width + j * quarter
+                    part = turned[start : start + quarter, lanes]
+                    extra = (high, low)[j][:, lanes] if j < 2 else jnp.zeros((1, LANES), F32)
+                    full = jnp.concatenate([part, jnp.broadcast_to(extra, (tail, LANES))], axis=0)
+                    stacked[at : at + block, j * LANES : (j + 1) * LANES] = full.astype(BF16)
+            swapped = dot(
+                stacked[base_at : base_at + chunk * block, :], swap, ((1,), (0,))
+            ).astype(BF16)
+            for d in range(chunk):
+                for b in range(groups):
+                    out_ref[(first + d) * owners + q * groups + b] = swapped[
+                        d * block : d * block + sent, b * LANES : (b + 1) * LANES
+                    ]
 
 
 def adam(old, first, second):
-    fixed = second * (1.0 / (1.0 - 0.999**10))
-    scale = fixed * lax.rsqrt(fixed) + 1e-08
-    return old - (0.05 / (1.0 - 0.9**10)) * first / scale
+    second_fix = (1.0 - 0.999**10) ** 0.5
+    scale = second * lax.rsqrt(second) + 1e-08 * second_fix
+    return old - (0.05 / (1.0 - 0.9**10) * second_fix) * first / scale
+
+
+def side_by_side(ref, first, count, groups):
+    return jnp.concatenate(
+        [
+            jnp.concatenate([ref[a * groups + b] for b in range(groups)], axis=1)
+            for a in range(first, first + count)
+        ],
+        axis=0,
+    )
 
 
 def update_kernel(
@@ -208,31 +221,33 @@
     load = pltpu.make_async_copy(old_two_hbm, two, load_sem)
     load.start()
     swap = swap_matrix(groups, capacity)
-    for a in range(tiles):
-        for b in range(groups):
-            stacked[a * block : a * block + sent, b * LANES : (b + 1) * LANES] = arrived_ref[
-                a * groups + b
-            ]
     down = lax.broadcasted_iota(jnp.int16, (rows_owned, LANES), 0)
     one_of, none_of = jnp.ones((rows_owned, LANES), BF16), jnp.zeros((rows_owned, LANES), BF16)
     id_row = sent - 1
-    for a in range(tiles):
-        lanes = slice(a * LANES, (a + 1) * LANES)
-        swapped = dot(stacked[a * block : (a + 1) * block, :], swap, ((1,), (0,)))
-        for j in range(groups):
-            turned[j * block : (j + 1) * block, lanes] = swapped[
-                :, j * LANES : (j + 1) * LANES
-            ].astype(BF16)
-        high = swapped[id_row : id_row + 1, 0:LANES].astype(jnp.int32)
-        low = swapped[id_row : id_row + 1, LANES : 2 * LANES].astype(jnp.int32)
-        ids = (lax.shift_left(high, base) + low).astype(jnp.int16)
-        hot[:, lanes] = jnp.where(down == ids, one_of, none_of)
-
-    def gather_rows(j, n):
+    for c in range(0, tiles, 4):
+        swapped = dot(side_by_side(arrived_ref, c, 4, groups), swap, ((1,), (0,)))
+        for a in range(4):
+            lanes = slice((c + a) * LANES, (c + a + 1) * LANES)
+            at = a * sent
+            for j in range(groups):
+                turned[j * block : j * block + sent, lanes] = swapped[
+                    at : at + sent, j * LANES : (j + 1) * LANES
+                ].astype(BF16)
+            ids_at = slice(at + id_row, at + id_row + 1)
+            high = swapped[ids_at, 0:LANES].astype(jnp.int32)
+            low = swapped[ids_at, LANES : 2 * LANES].astype(jnp.int32)
+            ids = (lax.shift_left(high, base) + low).astype(jnp.int16)
+            hot[:, lanes] = jnp.where(down == ids, one_of, none_of)
+
+    bands = 2
+    wide = groups // bands
+
+    def band(i):
+        return slice(i * wide * block, (i + 1) * wide * block)
+
+    def gather_rows(i, n):
         lanes = slice(n * span, (n + 1) * span)
-        total[j * block : (j + 1) * block, lanes] = dot(
-            turned[j * block : (j + 1) * block, :], hot[lanes, :], ((1,), (1,))
-        )
+        total[band(i), lanes] = dot(turned[band(i), :], hot[lanes, :], ((1,), (1,)))
 
     def step_rows(j, lanes):
         for top in range(0, quarter, 16):
@@ -249,17 +264,15 @@
                 new = jnp.concatenate([new, jnp.zeros((16 - size, LANES), F32)], axis=0)
             table[j * block + top : j * block + top + 16, lanes] = new.astype(BF16)
 
-    def look_rows(j, n):
-        looked = dot(
-            table[j * block : (j + 1) * block, :],
-            hot[:, n * span : (n + 1) * span],
-            ((1,), (0,)),
-        ).astype(BF16)
-        for h in range(2):
-            at = (2 * n + h) * block
-            stacked[at : at + block, j * LANES : (j + 1) * LANES] = looked[
-                :, h * LANES : (h + 1) * LANES
-            ]
+    def look_rows(i, n):
+        lanes = slice(n * span, (n + 1) * span)
+        looked = dot(table[band(i), :], hot[:, lanes], ((1,), (0,))).astype(BF16)
+        for j in range(wide):
+            for h in range(2):
+                at, to = (2 * n + h) * block, (i * wide + j) * LANES
+                stacked[at : at + block, to : to + LANES] = looked[
+                    j * block : (j + 1) * block, h * LANES : (h + 1) * LANES
+                ]
 
     pieces = sems.shape[1]
     height = slice_width // pieces
@@ -275,34 +288,40 @@
         for p in range(pieces)
     ]
     load.wait()
-    for n in range(rows_owned // span):
+    steps = rows_owned // span
+    looks = tiles // 2
+    for n in range(steps):
         gather_rows(0, n)
-    for j in range(groups + 1):
-        for n in range(max(rows_owned // span, tiles // 2)):
-            if j + 1 < groups and n < rows_owned // span:
-                gather_rows(j + 1, n)
-            if j > 0 and n < tiles // 2:
-                look_rows(j - 1, n)
-            if j < groups and n < rows_owned // span:
+    for i in range(bands + 1):
+        for n in range(max(steps, looks)):
+            if i + 1 < bands and n < steps:
+                gather_rows(i + 1, n)
+            if i > 0 and n < looks:
+                look_rows(i - 1, n)
+            if i < bands and n < steps:
                 for h in range(2):
-                    step_rows(j, slice((2 * n + h) * LANES, (2 * n + h + 1) * LANES))
-        if groups - pieces <= j < groups:
-            for copy in stores[j - groups + pieces]:
+                    for j in range(i * wide, (i + 1) * wide):
+                        step_rows(j, slice((2 * n + h) * LANES, (2 * n + h + 1) * LANES))
+        if bands - pieces <= i < bands:
+            for copy in stores[i - bands + pieces]:
                 copy.start()
-    for a in range(tiles):
-        back = dot(stacked[a * block : (a + 1) * block, :], swap, ((1,), (0,))).astype(BF16)
-        for b in range(groups):
-            out_ref[a * groups + b] = back[:quarter, b * LANES : (b + 1) * LANES]
+    for c in range(0, tiles, 4):
+        back = dot(stacked[c * block : (c + 4) * block, :], swap, ((1,), (0,))).astype(BF16)
+        for a in range(4):
+            for b in range(groups):
+                out_ref[(c + a) * groups + b] = back[
+                    a * block : a * block + quarter, b * LANES : (b + 1) * LANES
+                ]
     for piece in stores:
         for copy in piece:
             copy.wait()
 
 
-def place_kernel(dims, rows_ref, slots_ref, out_ref, stacked, turned):
+def place_kernel(dims, rows_ref, slots_ref, out_hbm, stacked, turned, placed, sems):
     n_dp, owners, capacity = dims
     groups = LANES // capacity
     quarter = rows_ref.shape[1]
-    width = out_ref.shape[1]
+    width = placed.shape[1]
     slice_width = width // n_dp
     block = stacked.shape[0] // (n_dp * (owners // groups))
     for q in range(owners // groups):
@@ -321,11 +340,25 @@
                 turned[start : start + quarter, q * LANES : (q + 1) * LANES] = swapped[
                     at : at + quarter, j * LANES : (j + 1) * LANES
                 ]
-    for k in range(0, width, 2 * LANES):
-        lanes = slice(k, min(k + 2 * LANES, width))
-        out_ref[:, lanes] = dot(
-            slots_ref[...], turned[lanes, :].astype(BF16), ((1,), (1,))
-        ).astype(BF16)
+    pieces = sems.shape[0]
+    span = width // pieces
+    copies = [
+        pltpu.make_async_copy(
+            placed.at[:, p * span : (p + 1) * span],
+            out_hbm.at[:, p * span : (p + 1) * span],
+            sems.at[p],
+        )
+        for p in range(pieces)
+    ]
+    for p, copy in enumerate(copies):
+        for k in range(p * span, (p + 1) * span, 2 * LANES):
+            lanes = slice(k, min(k + 2 * LANES, (p + 1) * span))
+            placed[:, lanes] = dot(
+                slots_ref[...], turned[lanes, :].astype(BF16), ((1,), (1,))
+            ).astype(BF16)
+        copy.start()
+    for copy in copies:
+        copy.wait()
 
 
 def per_device(token_ids, upstream, saved_rows, norm_gain, master, moment_one, moment_two):
@@ -341,7 +374,7 @@
     block = round_up(sent, 16)
     slots = owners * capacity
     stack = devices // groups * block
-    tile = 16
+    tile = 32
     base = 7
     full = pl.BlockSpec(memory_space=pltpu.VMEM)
 
@@ -366,7 +399,7 @@
             pltpu.VMEM((tokens, width), BF16),
             pltpu.VMEM((tokens, width), F32),
             pltpu.VMEM((tokens, width), F32),
-            pltpu.VMEM((4, tokens, LANES), F32),
+            pltpu.VMEM((3, tokens, LANES), F32),
             pltpu.VMEM((width, slots), F32),
             pltpu.VMEM((stack, groups * LANES), BF16),
             pltpu.SemaphoreType.DMA((2, tokens // tile)),
@@ -403,7 +436,7 @@
             pltpu.VMEM(state.shape, F32),
             pltpu.VMEM(state.shape, F32),
             pltpu.VMEM(state.shape, F32),
-            pltpu.SemaphoreType.DMA((3, groups if quarter % 8 == 0 else 1)),
+            pltpu.SemaphoreType.DMA((3, 2 if quarter % 4 == 0 else 1)),
             pltpu.SemaphoreType.DMA,
         ],
         compiler_params=params(28),
@@ -413,11 +446,13 @@
     new_rows = pl.pallas_call(
         functools.partial(place_kernel, (n_dp, owners, capacity)),
         in_specs=[full, full],
-        out_specs=full,
+        out_specs=hbm,
         out_shape=jax.ShapeDtypeStruct((tokens, width), BF16),
         scratch_shapes=[
             pltpu.VMEM((stack, groups * LANES), BF16),
             pltpu.VMEM((width, slots), F32),
+            pltpu.VMEM((tokens, width), BF16),
+            pltpu.SemaphoreType.DMA((3,)),
         ],
         compiler_params=params(16),
         name="place",

time: 98.1 us -> 96 us (0.979)
  Pallas kernels: 17.5 us -> 15.4 us
    pallas_call x1, Pallas kernels: 9.15 us -> 8.16 us  [per_device(): pl.pallas_call(functools.partial(update_kernel, (capacity, base)), in_spe...]
where the time goes in v3:
time: 96 us; the launch traced here: 95.8 us
  blocking collectives  79.7 us (83%)
  Pallas kernels  15.4 us (16%)
    all_to_all x1, blocking collectives, per_device(): lax.all_to_all(blocks, axes, split_axis=0, concat_axis=0, tiled=True)  42.9 us
    all_to_all x1, blocking collectives, per_device(): rows = lax.all_to_all(found, axes, split_axis=0, concat_axis=0, tiled=True)  36.9 us
    pallas_call x1, Pallas kernels, per_device(): pl.pallas_call(functools.partial(update_kernel, (capacity, base)), in_spe...  8.16 us
    pallas_call x1, Pallas kernels, per_device(): pl.pallas_call(functools.partial(send_kernel, (n_dp, owners, rows_owned,...  5.09 us
    pallas_call x1, Pallas kernels, per_device(): pl.pallas_call(functools.partial(place_kernel, (n_dp, owners, capacity)),...  2.18 us

profile of v3, /device:TPU:0, one launch (start us, length us, event | category | flops | bytes accessed | tf_op | source)
XLA Modules:
  0.0 95.8 jit_solution(4451130960809529380)
XLA Ops:
  0.6 0.0 copy-start.1
  0.6 5.1 %send.1 = (bf16[32,176,128]{2,1,0:T(8,128)(2,1)S(1)}, bf16[128,128]{1,0:T(8,128)(2,1)S(1)}) custom-call(s32[1,128]{1,0:T(1,128)} %ids_hbm.1, bf16[128,5376]{1,0:T(8,128)(2,1)} %bitcast.13, bf16[128,5376]{1,0:T(8,128)(2,1)} %bitcast.14, f32[42,128]{1,0:T(8,128)} %bitcast.16), custom_call_target="tpu_custom_call" | custom-call | tf_op jit(solution)/shard_map/send/pallas_call | solution.py:387
  5.7 0.0 copy-start
  5.8 42.9 %all_to_all.10.arrived_ref = bf16[32,176,128]{2,1,0:T(8,128)(2,1)S(1)} all-to-all(bf16[32,176,128]{2,1,0:T(8,128)(2,1)S(1)} %get-tuple-element.10), channel_id=1, replica_groups=mesh['dp'=8,'rows'=4] {'dp','rows'}, dimensions={0} | all-to-all | bytes 2883584 | tf_op jit(solution)/shard_map/all_to_all | solution.py:421
  48.6 0.0 copy-done.1
  48.6 0.0 copy-done
  48.6 8.2 %update.1 = (bf16[32,168,128]{2,1,0:T(8,128)(2,1)S(1)}, f32[672,1024]{1,0:T(8,128)}, f32[672,1024]{1,0:T(8,128)}, f32[672,1024]{1,0:T(8,128)}) custom-call(bf16[32,176,128]{2,1,0:T(8,128)(2,1)S(1)} %all_to_all.10.arrived_ref, f32[672,1024]{1,0:T(8,128)S(1)} %bitcast.10, f32[672,1024]{1,0:T(8,128)S(1)} %bitcast.11, f32[672,1024]{1,0:T(8,128)} %bitcast.12), custom_call_target="tpu_custom_call" | custom-call | tf_op jit(solution)/shard_map/update/pallas_call | solution.py:424
  56.8 36.9 %all_to_all.11.rows_ref = bf16[32,168,128]{2,1,0:T(8,128)(2,1)S(1)} all-to-all(bf16[32,168,128]{2,1,0:T(8,128)(2,1)S(1)} %get-tuple-element.14), channel_id=1, replica_groups=mesh['dp'=8,'rows'=4] {'dp','rows'}, dimensions={0} | all-to-all | bytes 2752512 | tf_op jit(solution)/shard_map/all_to_all | solution.py:445
  93.6 2.2 %place.1 = bf16[128,5376]{1,0:T(8,128)(2,1)} custom-call(bf16[32,168,128]{2,1,0:T(8,128)(2,1)S(1)} %all_to_all.11.rows_ref, bf16[128,128]{1,0:T(8,128)(2,1)S(1)} %get-tuple-element.15.slots_ref), custom_call_target="tpu_custom_call" | custom-call | tf_op jit(solution)/shard_map/place/pallas_call | solution.py:446
Async XLA Ops:
  0.6 48.0 %copy-start.1 = (f32[1024,672]{0,1:T(8,128)S(1)}, f32[1024,672]{0,1:T(8,128)}, u32[]{:S(2)}) copy-start(f32[1024,672]{0,1:T(8,128)} %param.12) | copy-start | bytes 8257540
  5.7 42.9 %copy-start = (f32[1024,672]{0,1:T(8,128)S(1)}, f32[1024,672]{0,1:T(8,128)}, u32[]{:S(2)}) copy-start(f32[1024,672]{0,1:T(8,128)} %param.11) | copy-start | bytes 8257540
